TPU v7x, 32 devices: a whole 2x2x4 slice. The times are simulated.
32 devices in a mesh: dp: 2 (over x), tm: 2 (over y), space: 8 (over z, core).
Axes of the slice: x: 2, y: 2, z: 4, core: 2. Of those that a mesh axis runs over, the one named last changes fastest.
Arguments:
- latents: bfloat16 [32, 4, 128, 512], P(('dp', 'tm', 'space')), parts along dimension 0, may hold values from -36 to 36, as said below
- norm_gain: float32 [512], replicated, may hold values from 0.1 to 1.9
- conv_weight: bfloat16 [3, 3, 3, 512, 256], replicated, may hold values from -0.0546875 to 0.0546875
- skip_weight: bfloat16 [512, 256], replicated, may hold values from -0.25 to 0.25
- cotangent: bfloat16 [32, 8, 4, 16, 256], P(('dp', 'tm'), 'space'), parts along dimension 0, may hold values from -6 to 6
Outputs:
- output: bfloat16 [32, 8, 4, 16, 256], P(('dp', 'tm'), 'space'), parts along dimension 0
- grad_input: bfloat16 [32, 8, 4, 16, 512], P(('dp', 'tm'), 'space'), parts along dimension 0
There are 2 independent parts, one for each index of `dp`. A program takes and returns all parts, laid end to end along the dimension named above; an argument that names none is the same for every part. Nothing has to cross between parts.
Inputs may be any that keep to these rules, and one draw needn't show every extreme that they name: `latents`: each cell and each channel has its own scale.
All inputs are finite; a program needn't handle non-finite values.
Results may differ from a plain program's by a relative error of at most 0.002.
Values may be sent and summed in bfloat16 or wider, within the bound.
No kernel may reach another device: no remote copies, remote signals or barrier semaphores. Data moves between devices by JAX's collectives and lax.ppermute only.
A program may use at most 192 MiB of HBM per device.

v0:
```python
import jax
import jax.numpy as jnp
from jax import lax
from jax.sharding import PartitionSpec as P

epsilon = 1e-06


def extended_2(block, sides, width):
    for axis, dim in sides:
        count = lax.axis_size(axis)
        forward = [(i, i + 1) for i in range(count - 1)]
        backward = [(target, source) for source, target in forward]
        low = lax.ppermute(
            lax.slice_in_dim(block, block.shape[dim] - width, None, axis=dim), axis, forward
        )
        high = lax.ppermute(lax.slice_in_dim(block, 0, width, axis=dim), axis, backward)
        block = jnp.concatenate([low, block, high], axis=dim)
    return block


def shifted(value, axis, steps):
    count = lax.axis_size(axis)
    first, last = (max(0, -steps), min(count, count - steps))
    return lax.ppermute(value, axis, [(source, source + steps) for source in range(first, last)])


def activate(x_float, norm_gain):
    mean_sq = jnp.mean(x_float * x_float, axis=-1, keepdims=True)
    inv_rms = lax.rsqrt(mean_sq + epsilon)
    unit_val = x_float * inv_rms
    return (inv_rms, unit_val, unit_val * norm_gain)


def silu_slope(normed):
    sigma_val = jax.nn.sigmoid(normed)
    return sigma_val * (1.0 + normed * (1.0 - sigma_val))


def framed_cut(frames_x, strips, tile_cols):
    frame_count, height, width, channels = frames_x.shape
    padded = jnp.pad(frames_x, ((0, 0), (1, 1), (1, 1), (0, 0)))
    left_cols = padded[:, :, 0:width:tile_cols]
    mid_cols = padded[:, :, 1 : width + 1].reshape(
        frame_count, height + 2, strips, tile_cols, channels
    )
    right_cols = padded[:, :, tile_cols + 1 : width + 2 : tile_cols]
    framed = jnp.concatenate([left_cols[:, :, :, None], mid_cols, right_cols[:, :, :, None]], 3)
    return framed.transpose(2, 0, 1, 3, 4)


def spread(field):
    widened = extended_2(field, (("space", 2),), 1)
    return jnp.pad(widened, ((0, 0), (1, 1), (0, 0), (0, 0)))


def local(latents, norm_gain, conv_weight, skip_weight, cotangent):
    strips = lax.axis_size("space")
    frame_count, height, width, in_chan = latents.shape
    group_len, single, tile_rows, tile_cols, out_chan = cotangent.shape
    outgoing = framed_cut(latents, strips, tile_cols)
    arrived = lax.all_to_all(outgoing, "space", split_axis=0, concat_axis=1, tiled=True)[0]
    inv_pad, unit_pad, normed_pad = activate(arrived.astype(jnp.float32), norm_gain)
    hidden_pad = jax.nn.silu(normed_pad).astype(jnp.bfloat16)
    inv_rms = inv_pad[:, 1:-1, 1:-1]
    unit_val = unit_pad[:, 1:-1, 1:-1]
    normed = normed_pad[:, 1:-1, 1:-1]
    tile_x = arrived[:, 1:-1, 1:-1]
    past_rows = shifted(hidden_pad[group_len - 2 :], "tm", 1)
    extended = jnp.concatenate([past_rows, hidden_pad], 0)
    summed = jnp.dot(tile_x.reshape(-1, in_chan), skip_weight, preferred_element_type=jnp.float32)
    for t_tap in range(3):
        for h_tap in range(3):
            for w_tap in range(3):
                window = extended[
                    t_tap : t_tap + group_len, h_tap : h_tap + tile_rows, w_tap : w_tap + tile_cols
                ]
                summed = summed + jnp.dot(
                    window.reshape(-1, in_chan),
                    conv_weight[t_tap, h_tap, w_tap],
                    preferred_element_type=jnp.float32,
                )
    output = summed.astype(jnp.bfloat16).reshape(group_len, 1, tile_rows, tile_cols, out_chan)
    grad_out = cotangent[:, 0]
    grad_pad = spread(grad_out)
    next_rows = shifted(grad_pad[0:2], "tm", -1)
    grad_ext = jnp.concatenate([grad_pad, next_rows], 0)
    contract = (((1,), (1,)), ((), ()))
    grad_skip = lax.dot_general(
        grad_out.reshape(-1, out_chan), skip_weight, contract, preferred_element_type=jnp.float32
    )
    grad_hidden = jnp.zeros((group_len * tile_rows * tile_cols, in_chan), jnp.float32)
    for t_tap in range(3):
        for h_tap in range(3):
            for w_tap in range(3):
                window = grad_ext[
                    2 - t_tap : 2 - t_tap + group_len,
                    2 - h_tap : 2 - h_tap + tile_rows,
                    2 - w_tap : 2 - w_tap + tile_cols,
                ]
                grad_hidden = grad_hidden + lax.dot_general(
                    window.reshape(-1, out_chan),
                    conv_weight[t_tap, h_tap, w_tap],
                    contract,
                    preferred_element_type=jnp.float32,
                )
    grad_unit = (
        grad_hidden.reshape(group_len, tile_rows, tile_cols, in_chan)
        * silu_slope(normed)
        * norm_gain
    )
    grad_input = inv_rms * (
        grad_unit - unit_val * jnp.mean(grad_unit * unit_val, axis=-1, keepdims=True)
    )
    grad_input = grad_input + grad_skip.reshape(group_len, tile_rows, tile_cols, in_chan)
    return (
        output,
        grad_input.astype(jnp.bfloat16).reshape(group_len, 1, tile_rows, tile_cols, in_chan),
    )


def solution(mesh):
    placed = (
        P(("dp", "tm", "space"), None, None, None),
        P(),
        P(),
        P(),
        P(("dp", "tm"), "space", None, None, None),
    )
    return jax.shard_map(
        local,
        mesh=mesh,
        in_specs=placed,
        out_specs=(
            P(("dp", "tm"), "space", None, None, None),
            P(("dp", "tm"), "space", None, None, None),
        ),
        check_vma=False,
    )
```

profile of v0, /device:TPU:0, one launch (start us, length us, event | category | flops | bytes accessed | tf_op | source)
XLA Modules:
  0.0 74.0 jit_solution(17573924246514559045)
XLA Ops:
  0.7 1.1 %fusion.230 = (bf16[8,4,1,256]{3,2,1,0:T(2,128)(2,1)S(1)}, bf16[8,4,1,256]{3,2,1,0:T(2,128)(2,1)S(1)}) fusion(bf16[8,4,16,256]{3,2,1,0:T(8,128)(2,1)} %bitcast.283), kind=kLoop, calls=%fused_computation.333 | loop fusion | bytes 65536 | tf_op jit(solution)/shard_map/slice | solution.py:15
  1.7 2.4 %collective-permute-start.1 = (bf16[8,4,1,256]{3,2,1,0:T(2,128)(2,1)S(1)}, bf16[8,4,1,256]{3,2,1,0:T(2,128)(2,1)S(1)}, u32[]{:S(2)}, u32[]{:S(2)}) collective-permute-start(bf16[8,4,1,256]{3,2,1,0:T(2,128)(2,1)S(1)} %get-tuple-element.66), channel_id=1, source_target_pairs={{0,1},{1,2},{2,3},{3,4},{4,5},{5,6},{6,7},{8,9},{9,10},{10,11},{11... | collective-permute-start | bytes 49160 | tf_op jit(solution)/shard_map/ppermute | solution.py:14
  4.1 1.3 %collective-permute-start.2 = (bf16[8,4,1,256]{3,2,1,0:T(2,128)(2,1)S(1)}, bf16[8,4,1,256]{3,2,1,0:T(2,128)(2,1)S(1)}, u32[]{:S(2)}, u32[]{:S(2)}) collective-permute-start(bf16[8,4,1,256]{3,2,1,0:T(2,128)(2,1)S(1)} %get-tuple-element.67), channel_id=1, source_target_pairs={{1,0},{2,1},{3,2},{4,3},{5,4},{6,5},{7,6},{9,8},{10,9},{11,10},{12... | collective-permute-start | bytes 49160 | tf_op jit(solution)/shard_map/ppermute | solution.py:17
  5.4 1.2 %pad.8 = bf16[1,6,130,512]{3,2,1,0:T(8,128)(2,1)S(1)} pad(bf16[1,4,128,512]{3,2,1,0:T(8,128)(2,1)} %param.5, bf16[]{:T(256)} %constant.5.clone.1), padding=0_0x1_1x1_1x0_0 | pad | bytes 1323010 | tf_op jit(solution)/shard_map/jit(_pad)/pad | solution.py:42
  6.8 1.1 %pad_slice_fusion.68 = bf16[1,6,128,512]{3,2,1,0:T(8,128)(2,1)S(1)} fusion(bf16[1,4,128,512]{3,2,1,0:T(8,128)(2,1)} %param.5), kind=kLoop, calls=%fused_computation.325 | loop fusion | bytes 1310720 | tf_op jit(solution)/shard_map/slice | solution.py:44
  8.8 1.1 %copy.24 = bf16[8,1,6,18,512]{4,3,2,1,0:T(8,128)(2,1)} copy(bf16[8,1,6,18,512]{4,3,0,2,1:T(8,128)(2,1)S(1)} %maximum_bitcast_fusion) | data formatting | bytes 1769472 | tf_op jit(solution)/shard_map/transpose | solution.py:49
  10.0 8.5 %all-to-all-start = ((bf16[8,1,6,18,512]{4,3,2,1,0:T(8,128)(2,1)}), bf16[8,1,6,18,512]{4,3,2,1,0:T(8,128)(2,1)}, u32[]{:S(2)}, u32[]{:S(2)}) async-start(bf16[8,1,6,18,512]{4,3,2,1,0:T(8,128)(2,1)} %copy.24), calls=%async_computation | async-start | bytes 2359296 | tf_op jit(solution)/shard_map/all_to_all | solution.py:62
  18.4 1.3 %fusion.90 = f32[512,512]{1,0:T(8,128)S(1)} fusion(bf16[512,256]{1,0:T(8,128)(2,1)S(1)} %bitcast.284, bf16[3,3,3,512,256]{4,3,2,1,0:T(8,128)(2,1)} %param.7), kind=kOutput, calls=%fused_computation.189 | convolution fusion | flops 134217728 | bytes 1572864 | tf_op jit(solution)/shard_map/dot_general | solution.py:101
  20.2 1.3 %collective-permute-start.3 = (bf16[2,6,18,256]{3,2,1,0:T(8,128)(2,1)S(1)}, bf16[2,6,18,256]{3,2,1,0:T(8,128)(2,1)S(1)}, u32[]{:S(2)}, u32[]{:S(2)}) collective-permute-start(bf16[2,6,18,256]{3,2,1,0:T(8,128)(2,1)S(1)} %slice.445), channel_id=1, source_target_pairs={{8,0},{9,1},{10,2},{11,3},{12,4},{13,5},{14,6},{15,7},{24,16},{25,... | collective-permute-start | bytes 331784 | tf_op jit(solution)/shard_map/ppermute | solution.py:25
  21.6 1.4 %fusion.99 = f32[512,512]{1,0:T(8,128)S(1)} fusion(bf16[512,256]{1,0:T(8,128)(2,1)S(1)} %bitcast.340, bf16[3,3,3,512,256]{4,3,2,1,0:T(8,128)(2,1)} %param.7), kind=kOutput, calls=%fused_computation.198 | convolution fusion | flops 134217728 | bytes 1572864 | tf_op jit(solution)/shard_map/dot_general | solution.py:101
  23.0 1.3 %fusion.85 = f32[512,512]{1,0:T(8,128)S(1)} fusion(bf16[512,256]{1,0:T(8,128)(2,1)S(1)} %bitcast.339, bf16[3,3,3,512,256]{4,3,2,1,0:T(8,128)(2,1)} %param.7), kind=kOutput, calls=%fused_computation.184 | convolution fusion | flops 134217728 | bytes 1572864 | tf_op jit(solution)/shard_map/dot_general | solution.py:101
  24.5 3.9 %collective-permute-done.3 = bf16[2,6,18,256]{3,2,1,0:T(8,128)(2,1)S(1)} collective-permute-done((bf16[2,6,18,256]{3,2,1,0:T(8,128)(2,1)S(1)}, bf16[2,6,18,256]{3,2,1,0:T(8,128)(2,1)S(1)}, u32[]{:S(2)}, u32[]{:S(2)}) %collective-permute-start.3) | collective-permute-done | bytes 110624 | tf_op jit(solution)/shard_map/ppermute | solution.py:25
  34.8 1.7 %fusion.19 = f32[512,512]{1,0:T(8,128)S(1)} fusion(f32[512,512]{1,0:T(8,128)S(1)} %fusion.99, f32[512,512]{1,0:T(8,128)S(1)} %fusion.103, f32[512,512]{1,0:T(8,128)S(1)} %fusion.107, f32[512,512]{1,0:T(8,128)S(1)} %fusion.111, f32[512,512]{1,0:T(8,128)S(1)} %fusion.115, f32[512,512]{1,0:T(8,128)S(1)} %fusion.119, f32[512,512]{1,0:T(8,128)S(1)} %fusion.123, ...), kind=kOutput, calls=%fused_computation.66 | convolution fusion | flops 138936320 | bytes 20447232 | tf_op jit(solution)/shard_map/dot_general | solution.py:101
  38.2 1.3 %convolution_add_fusion.1 = f32[512,512]{1,0:T(8,128)} fusion(f32[512,512]{1,0:T(8,128)S(1)} %convolution_add_fusion.2, bf16[512,256]{1,0:T(8,128)(2,1)S(1)} %bitcast.319, bf16[3,3,3,512,256]{4,3,2,1,0:T(8,128)(2,1)S(1)} %bitcast.277), kind=kOutput, calls=%fused_computation.41 | convolution fusion | flops 134479872 | bytes 2621440 | tf_op jit(solution)/shard_map/dot_general | solution.py:101
  39.6 8.4 %all-to-all-done = bf16[8,1,6,18,512]{4,3,2,1,0:T(8,128)(2,1)} async-done(((bf16[8,1,6,18,512]{4,3,2,1,0:T(8,128)(2,1)}), bf16[8,1,6,18,512]{4,3,2,1,0:T(8,128)(2,1)}, u32[]{:S(2)}, u32[]{:S(2)}) %all-to-all-start) | async-done | bytes 884768 | tf_op jit(solution)/shard_map/all_to_all | solution.py:62
  47.9 1.6 %fusion = f32[8,6,18]{2,1,0:T(8,128)S(1)} fusion(bf16[8,1,6,18,512]{4,3,2,1,0:T(8,128)(2,1)} %all-to-all-done), kind=kLoop, calls=%fused_computation.36 | loop fusion | flops 1326240 | bytes 888192 | tf_op jit(solution)/shard_map/reduce_sum | solution.py:29
  49.6 2.1 %broadcast_multiply_fusion = (f32[8,6,18,512]{3,2,1,0:T(8,128)S(1)}, bf16[8,6,18,512]{3,2,1,0:T(8,128)(2,1)S(1)}, f32[8,6,18,512]{3,2,1,0:T(8,128)S(1)}) fusion(f32[512]{0:T(512)S(1)} %copy-done.3, f32[8,6,18]{2,1,0:T(8,128)S(1)} %get-tuple-element.69, bf16[8,1,6,18,512]{4,3,2,1,0:T(8,128)(2,1)} %all-to-all-done), kind=kLoop, calls=%fused_computation.98 | loop fusion | flops 3538944 | bytes 5313920 | tf_op jit(solution)/shard_map/mul | solution.py:32
  53.1 3.7 %collective-permute-start = (bf16[2,6,18,512]{3,2,1,0:T(8,128)(2,1)S(1)}, bf16[2,6,18,512]{3,2,1,0:T(8,128)(2,1)S(1)}, u32[]{:S(2)}, u32[]{:S(2)}) collective-permute-start(bf16[2,6,18,512]{3,2,1,0:T(8,128)(2,1)S(1)} %slice.398), channel_id=1, source_target_pairs={{0,8},{1,9},{2,10},{3,11},{4,12},{5,13},{6,14},{7,15},{16,24},{17,... | collective-permute-start | bytes 663560 | tf_op jit(solution)/shard_map/ppermute | solution.py:25
  56.8 1.3 %slice.397 = bf16[8,4,16,512]{3,2,1,0:T(8,128)(2,1)S(1)} slice(bf16[8,6,18,512]{3,2,1,0:T(8,128)(2,1)} %bitcast.4), slice={[0:8], [1:5], [1:17], [0:512]} | slice | bytes 1048576 | tf_op jit(solution)/shard_map/slice | solution.py:68
  58.5 1.6 %fusion.21 = bf16[8,1,4,16,512]{4,3,2,1,0:T(8,128)(2,1)} fusion(f32[8,6,18,512]{3,2,1,0:T(8,128)S(1)} %get-tuple-element.30, f32[8,4,16]{2,1,0:T(4,128)S(1)} %broadcast_multiply_fusion.1, f32[8,4,16]{2,1,0:T(4,128)S(1)} %slice_bitcast_fusion, bf16[512,256]{1,0:T(8,128)(2,1)S(1)} %copy-done, bf16[8,1,4,16,256]{4,3,2,1,0:T(8,128)(2,1)S(1)} %copy-done.2, ...), kind=kOutput, calls=%fused_computation.68 | convolution fusion | flops 137887744 | bytes 4200448 | tf_op jit(solution)/shard_map/dot_general | solution.py:89
  60.6 2.0 %collective-permute-done = bf16[2,6,18,512]{3,2,1,0:T(8,128)(2,1)S(1)} collective-permute-done((bf16[2,6,18,512]{3,2,1,0:T(8,128)(2,1)S(1)}, bf16[2,6,18,512]{3,2,1,0:T(8,128)(2,1)S(1)}, u32[]{:S(2)}, u32[]{:S(2)}) %collective-permute-start) | collective-permute-done | bytes 221216 | tf_op jit(solution)/shard_map/ppermute | solution.py:25
  62.6 1.1 %fusion.48 = (bf16[8,4,16,512]{3,2,1,0:T(8,128)(2,1)S(1)}, bf16[8,4,16,512]{3,2,1,0:T(8,128)(2,1)S(1)}, bf16[8,4,16,512]{3,2,1,0:T(8,128)(2,1)S(1)}, bf16[8,4,16...) fusion(bf16[8,6,18,512]{3,2,1,0:T(8,128)(2,1)S(1)} %get-tuple-e, ...), kind=kLoop, calls=%fused_computation.126 | loop fusion | flops 2359296 | bytes 7241728 | tf_op jit(solution)/shard_map/concatenate | solution.py:70
  65.8 1.3 %fusion.56 = (bf16[8,4,16,512]{3,2,1,0:T(8,128)(2,1)S(1)}, bf16[8,4,16,512]{3,2,1,0:T(8,128)(2,1)S(1)}, bf16[8,4,16,512]{3,2,1,0:T(8,128)(2,1)S(1)}, bf16[8,4,16...) fusion(bf16[8,6,18,512]{3,2,1,0:T(8,128)(2,1)S(1)} %get-tuple-e, ...), kind=kLoop, calls=%fused_computation.134 | loop fusion | flops 9437184 | bytes 7241728 | tf_op jit(solution)/shard_map/concatenate | solution.py:70
  73.0 1.0 %fusion.39 = bf16[512,256]{1,0:T(8,128)(2,1)} fusion(f32[512,256]{1,0:T(8,128)S(1)} %convolution_add_fusion.9, bf16[512,512]{1,0:T(8,128)(2,1)S(1)} %bitcast.294, bf16[3,3,3,512,256]{4,3,2,1,0:T(8,128)(2,1)S(1)} %bitcast.279), kind=kOutput, calls=%fused_computation.96 | convolution fusion | flops 134479872 | bytes 1572864 | tf_op jit(solution)/shard_map/dot_general | solution.py:78
  (86 shorter events, 19.6 us)
Async XLA Ops:
  0.6 57.5 %copy-start = (bf16[512,256]{1,0:T(8,128)(2,1)S(1)}, bf16[512,256]{1,0:T(8,128)(2,1)}, u32[]{:S(2)}) copy-start(bf16[512,256]{1,0:T(8,128)(2,1)} %param.8) | copy-start | bytes 786436
  0.6 17.8 %copy-start.2 = (bf16[8,1,4,16,256]{4,3,2,1,0:T(8,128)(2,1)S(1)}, bf16[8,1,4,16,256]{4,3,2,1,0:T(8,128)(2,1)}, u32[]{:S(2)}) copy-start(bf16[8,1,4,16,256]{4,3,2,1,0:T(8,128)(2,1)} %param.9) | copy-start | bytes 786436
  1.7 18.0 %collective-permute-start.1 = (bf16[8,4,1,256]{3,2,1,0:T(2,128)(2,1)S(1)}, bf16[8,4,1,256]{3,2,1,0:T(2,128)(2,1)S(1)}, u32[]{:S(2)}, u32[]{:S(2)}) collective-permute-start(bf16[8,4,1,256]{3,2,1,0:T(2,128)(2,1)S(1)} %get-tuple-element.66), channel_id=1, source_target_pairs={{0,1},{1,2},{2,3},{3,4},{4,5},{5,6},{6,7},{8,9},{9,10},{10,11},{11... | collective-permute-start | bytes 49160 | tf_op jit(solution)/shard_map/ppermute | solution.py:14
  4.1 15.6 %collective-permute-start.2 = (bf16[8,4,1,256]{3,2,1,0:T(2,128)(2,1)S(1)}, bf16[8,4,1,256]{3,2,1,0:T(2,128)(2,1)S(1)}, u32[]{:S(2)}, u32[]{:S(2)}) collective-permute-start(bf16[8,4,1,256]{3,2,1,0:T(2,128)(2,1)S(1)} %get-tuple-element.67), channel_id=1, source_target_pairs={{1,0},{2,1},{3,2},{4,3},{5,4},{6,5},{7,6},{9,8},{10,9},{11,10},{12... | collective-permute-start | bytes 49160 | tf_op jit(solution)/shard_map/ppermute | solution.py:17
  10.0 18.9 %slice-start = ((s8[7077888]{0:T(1024)(128)(4,1)}), s8[2883584]{0:T(1024)(128)(4,1)S(1)}, s32[]{:S(2)}) async-start(s8[7077888]{0:T(1024)(128)(4,1)} %bitcast.276), calls=%async_computation.1 | async-start | bytes 5767168
  10.0 38.0 %all-to-all-start = ((bf16[8,1,6,18,512]{4,3,2,1,0:T(8,128)(2,1)}), bf16[8,1,6,18,512]{4,3,2,1,0:T(8,128)(2,1)}, u32[]{:S(2)}, u32[]{:S(2)}) async-start(bf16[8,1,6,18,512]{4,3,2,1,0:T(8,128)(2,1)} %copy.24), calls=%async_computation | async-start | bytes 2359296 | tf_op jit(solution)/shard_map/all_to_all | solution.py:62
  20.2 8.2 %collective-permute-start.3 = (bf16[2,6,18,256]{3,2,1,0:T(8,128)(2,1)S(1)}, bf16[2,6,18,256]{3,2,1,0:T(8,128)(2,1)S(1)}, u32[]{:S(2)}, u32[]{:S(2)}) collective-permute-start(bf16[2,6,18,256]{3,2,1,0:T(8,128)(2,1)S(1)} %slice.445), channel_id=1, source_target_pairs={{8,0},{9,1},{10,2},{11,3},{12,4},{13,5},{14,6},{15,7},{24,16},{25,... | collective-permute-start | bytes 331784 | tf_op jit(solution)/shard_map/ppermute | solution.py:25
  21.5 7.4 %slice-start.1 = ((s8[7077888]{0:T(1024)(128)(4,1)}), s8[4194304]{0:T(1024)(128)(4,1)S(1)}, s32[]{:S(2)}) async-start(s8[7077888]{0:T(1024)(128)(4,1)} %bitcast.276), calls=%async_computation.2 | async-start | bytes 8388608
  37.1 12.4 %copy-start.3 = (f32[512]{0:T(512)S(1)}, f32[512]{0:T(512)}, u32[]{:S(2)}) copy-start(f32[512]{0:T(512)} %param.6) | copy-start | bytes 6148
  49.6 2.8 %copy-start.1 = (f32[512,512]{1,0:T(8,128)S(1)}, f32[512,512]{1,0:T(8,128)}, u32[]{:S(2)}) copy-start(f32[512,512]{1,0:T(8,128)} %convolution_add_fusion.1) | copy-start | bytes 3145732
  52.3 7.8 %slice-start.2 = ((s8[7077888]{0:T(1024)(128)(4,1)}), s8[4194304]{0:T(1024)(128)(4,1)S(1)}, s32[]{:S(2)}) async-start(s8[7077888]{0:T(1024)(128)(4,1)} %bitcast.278), calls=%async_computation.3 | async-start | bytes 8388608
  53.1 9.5 %collective-permute-start = (bf16[2,6,18,512]{3,2,1,0:T(8,128)(2,1)S(1)}, bf16[2,6,18,512]{3,2,1,0:T(8,128)(2,1)S(1)}, u32[]{:S(2)}, u32[]{:S(2)}) collective-permute-start(bf16[2,6,18,512]{3,2,1,0:T(8,128)(2,1)S(1)} %slice.398), channel_id=1, source_target_pairs={{0,8},{1,9},{2,10},{3,11},{4,12},{5,13},{6,14},{7,15},{16,24},{17,... | collective-permute-start | bytes 663560 | tf_op jit(solution)/shard_map/ppermute | solution.py:25
  58.4 1.8 %slice-start.3 = ((s8[7077888]{0:T(1024)(128)(4,1)}), s8[2883584]{0:T(1024)(128)(4,1)S(1)}, s32[]{:S(2)}) async-start(s8[7077888]{0:T(1024)(128)(4,1)} %bitcast.278), calls=%async_computation.4 | async-start | bytes 5767168
where the time goes:
time: 74.5 us; the launch traced here: 74 us
  matrix products  25.2 us (34%)
  starting transfers between devices  17.2 us (23%)
  waiting for transfers between devices  14.3 us (19%)
  other arithmetic  8.74 us (12%)
  local copies, waits for them, and re-layouts  7.31 us (10%)
  between operations  1.28 us (2%)
    dot_general x27, matrix products, local(): lax.dot_general(window.reshape(-1, out_chan), conv_weight[t_tap, h_tap, w...  14.2 us
    dot_general x27, matrix products, local(): jnp.dot(window.reshape(-1, in_chan), conv_weight[t_tap, h_tap, w_tap], pr...  9 us
    all_to_all x1, starting transfers between devices, local(): lax.all_to_all(outgoing, 'space', split_axis=0, concat_axis=1, tiled=True)  8.49 us
    all_to_all x1, waiting for transfers between devices, local(): lax.all_to_all(outgoing, 'space', split_axis=0, concat_axis=1, tiled=True)  8.37 us
    ppermute x2, waiting for transfers between devices, shifted(): lax.ppermute(value, axis, [(source, source + steps) for source in range(f...  5.89 us
    ppermute x2, starting transfers between devices, shifted(): lax.ppermute(value, axis, [(source, source + steps) for source in range(f...  5.04 us
    concatenate x2, other arithmetic, local(): extended = jnp.concatenate([past_rows, hidden_pad], 0)  2.48 us
    ppermute x1, starting transfers between devices, extended_2(): lax.ppermute(lax.slice_in_dim(block, block.shape[dim] - width, None, axis...  2.4 us
  transfers between devices with their start and end apart: 5, of which 3 were waited for; matrix products, arithmetic and copies ran while one was open for 32% of the time, Pallas kernels for 0%

commit v1 on v0

--- a/solution.py
+++ b/solution.py
@@ -4,6 +4,13 @@
 from jax.sharding import PartitionSpec as P
 
 epsilon = 1e-06
+
+
+def exchange_blocks(x, axis, split, join):
+    devices = lax.axis_size(axis)
+    tiles = jnp.stack(jnp.split(x, devices, axis=split), axis=0)
+    tiles = lax.all_to_all(tiles, axis, split_axis=0, concat_axis=0)
+    return jnp.concatenate(tiles, axis=join)
 
 
 def extended_2(block, sides, width):
@@ -59,7 +66,7 @@
     frame_count, height, width, in_chan = latents.shape
     group_len, single, tile_rows, tile_cols, out_chan = cotangent.shape
     outgoing = framed_cut(latents, strips, tile_cols)
-    arrived = lax.all_to_all(outgoing, "space", split_axis=0, concat_axis=1, tiled=True)[0]
+    arrived = exchange_blocks(outgoing, "space", 0, 1)[0]
     inv_pad, unit_pad, normed_pad = activate(arrived.astype(jnp.float32), norm_gain)
     hidden_pad = jax.nn.silu(normed_pad).astype(jnp.bfloat16)
     inv_rms = inv_pad[:, 1:-1, 1:-1]

time: 74.5 us -> 79.2 us (1.063)
  local copies, waits for them, and re-layouts: 7.31 us -> 12.2 us
    unnamed x16 -> x23, local copies, waits for them, and re-layouts: 0.22 us -> 5.63 us
    transpose x1 -> x0, local copies, waits for them, and re-layouts: 1.13 us -> none  [framed_cut(): return framed.transpose(2, 0, 1, 3, 4)]
  transfers between devices with their start and end apart: 5 -> 5, of which waited for: 3 -> 3; matrix products, arithmetic and copies ran while one was open for 32% -> 35% of each run, Pallas kernels for 0% -> 0%
where the time goes in v1:
time: 79.2 us; the launch traced here: 78.7 us
  matrix products  25.3 us (32%)
  starting transfers between devices  17.2 us (22%)
  waiting for transfers between devices  14.1 us (18%)
  local copies, waits for them, and re-layouts  12.2 us (15%)
  other arithmetic  8.51 us (11%)
  between operations  1.27 us (2%)
    dot_general x27, matrix products, local(): lax.dot_general(window.reshape(-1, out_chan), conv_weight[t_tap, h_tap, w...  14.2 us
    dot_general x27, matrix products, local(): jnp.dot(window.reshape(-1, in_chan), conv_weight[t_tap, h_tap, w_tap], pr...  9.16 us
    all_to_all x1, starting transfers between devices, exchange_blocks(): tiles = lax.all_to_all(tiles, axis, split_axis=0, concat_axis=0)  8.49 us
    all_to_all x1, waiting for transfers between devices, exchange_blocks(): tiles = lax.all_to_all(tiles, axis, split_axis=0, concat_axis=0)  8.37 us
    ppermute x2, waiting for transfers between devices, shifted(): lax.ppermute(value, axis, [(source, source + steps) for source in range(f...  5.77 us
    unnamed x23, local copies, waits for them, and re-layouts  5.63 us
    ppermute x2, starting transfers between devices, shifted(): lax.ppermute(value, axis, [(source, source + steps) for source in range(f...  5.04 us
    ppermute x1, starting transfers between devices, extended_2(): lax.ppermute(lax.slice_in_dim(block, block.shape[dim] - width, None, axis...  2.4 us
  transfers between devices with their start and end apart: 5, of which 3 were waited for; matrix products, arithmetic and copies ran while one was open for 35% of the time, Pallas kernels for 0%

profile of v1, /device:TPU:0, one launch (start us, length us, event | category | flops | bytes accessed | tf_op | source)
XLA Modules:
  0.0 78.7 jit_solution(3330312876080209239)
XLA Ops:
  0.6 1.1 %fusion.238 = (bf16[8,4,1,256]{3,2,1,0:T(2,128)(2,1)S(1)}, bf16[8,4,1,256]{3,2,1,0:T(2,128)(2,1)S(1)}) fusion(bf16[8,4,16,256]{3,2,1,0:T(8,128)(2,1)} %bitcast.329), kind=kLoop, calls=%fused_computation.349 | loop fusion | bytes 65536 | tf_op jit(solution)/shard_map/slice | solution.py:22
  1.7 2.4 %collective-permute-start.1 = (bf16[8,4,1,256]{3,2,1,0:T(2,128)(2,1)S(1)}, bf16[8,4,1,256]{3,2,1,0:T(2,128)(2,1)S(1)}, u32[]{:S(2)}, u32[]{:S(2)}) collective-permute-start(bf16[8,4,1,256]{3,2,1,0:T(2,128)(2,1)S(1)} %get-tuple-element.66), channel_id=1, source_target_pairs={{0,1},{1,2},{2,3},{3,4},{4,5},{5,6},{6,7},{8,9},{9,10},{10,11},{11... | collective-permute-start | bytes 49160 | tf_op jit(solution)/shard_map/ppermute | solution.py:21
  4.1 1.3 %collective-permute-start.2 = (bf16[8,4,1,256]{3,2,1,0:T(2,128)(2,1)S(1)}, bf16[8,4,1,256]{3,2,1,0:T(2,128)(2,1)S(1)}, u32[]{:S(2)}, u32[]{:S(2)}) collective-permute-start(bf16[8,4,1,256]{3,2,1,0:T(2,128)(2,1)S(1)} %get-tuple-element.67), channel_id=1, source_target_pairs={{1,0},{2,1},{3,2},{4,3},{5,4},{6,5},{7,6},{9,8},{10,9},{11,10},{12... | collective-permute-start | bytes 49160 | tf_op jit(solution)/shard_map/ppermute | solution.py:24
  5.4 1.2 %pad.8 = bf16[1,6,130,512]{3,2,1,0:T(8,128)(2,1)S(1)} pad(bf16[1,4,128,512]{3,2,1,0:T(8,128)(2,1)} %param.5, bf16[]{:T(256)} %constant.5.clone.1), padding=0_0x1_1x1_1x0_0 | pad | bytes 1323010 | tf_op jit(solution)/shard_map/jit(_pad)/pad | solution.py:49
  6.8 1.1 %pad_slice_fusion.68 = bf16[1,6,128,512]{3,2,1,0:T(8,128)(2,1)S(1)} fusion(bf16[1,4,128,512]{3,2,1,0:T(8,128)(2,1)} %param.5), kind=kLoop, calls=%fused_computation.341 | loop fusion | bytes 1310720 | tf_op jit(solution)/shard_map/slice | solution.py:51
  14.1 8.5 %all-to-all-start = ((bf16[8,1,1,6,18,512]{5,4,3,2,1,0:T(8,128)(2,1)}), bf16[8,1,1,6,18,512]{5,4,3,2,1,0:T(8,128)(2,1)}, u32[]{:S(2)}, u32[]{:S(2)}) async-start(bf16[8,1,1,6,18,512]{5,4,3,2,1,0:T(8,128)(2,1)} %fusion.226), calls=%async_computation | async-start | bytes 2359296 | tf_op jit(solution)/shard_map/all_to_all | solution.py:12
  22.6 1.3 %fusion.90 = f32[512,512]{1,0:T(8,128)S(1)} fusion(bf16[512,256]{1,0:T(8,128)(2,1)S(1)} %bitcast.330, bf16[3,3,3,512,256]{4,3,2,1,0:T(8,128)(2,1)} %param.7), kind=kOutput, calls=%fused_computation.189 | convolution fusion | flops 134217728 | bytes 1572864 | tf_op jit(solution)/shard_map/dot_general | solution.py:108
  24.4 1.3 %collective-permute-start.3 = (bf16[2,6,18,256]{3,2,1,0:T(8,128)(2,1)S(1)}, bf16[2,6,18,256]{3,2,1,0:T(8,128)(2,1)S(1)}, u32[]{:S(2)}, u32[]{:S(2)}) collective-permute-start(bf16[2,6,18,256]{3,2,1,0:T(8,128)(2,1)S(1)} %slice.445), channel_id=1, source_target_pairs={{8,0},{9,1},{10,2},{11,3},{12,4},{13,5},{14,6},{15,7},{24,16},{25,... | collective-permute-start | bytes 331784 | tf_op jit(solution)/shard_map/ppermute | solution.py:32
  25.7 1.4 %fusion.99 = f32[512,512]{1,0:T(8,128)S(1)} fusion(bf16[512,256]{1,0:T(8,128)(2,1)S(1)} %bitcast.386, bf16[3,3,3,512,256]{4,3,2,1,0:T(8,128)(2,1)} %param.7), kind=kOutput, calls=%fused_computation.198 | convolution fusion | flops 134217728 | bytes 1572864 | tf_op jit(solution)/shard_map/dot_general | solution.py:108
  27.2 1.3 %fusion.85 = f32[512,512]{1,0:T(8,128)S(1)} fusion(bf16[512,256]{1,0:T(8,128)(2,1)S(1)} %bitcast.385, bf16[3,3,3,512,256]{4,3,2,1,0:T(8,128)(2,1)} %param.7), kind=kOutput, calls=%fused_computation.184 | convolution fusion | flops 134217728 | bytes 1572864 | tf_op jit(solution)/shard_map/dot_general | solution.py:108
  28.7 3.9 %collective-permute-done.3 = bf16[2,6,18,256]{3,2,1,0:T(8,128)(2,1)S(1)} collective-permute-done((bf16[2,6,18,256]{3,2,1,0:T(8,128)(2,1)S(1)}, bf16[2,6,18,256]{3,2,1,0:T(8,128)(2,1)S(1)}, u32[]{:S(2)}, u32[]{:S(2)}) %collective-permute-start.3) | collective-permute-done | bytes 110624 | tf_op jit(solution)/shard_map/ppermute | solution.py:32
  39.0 1.7 %fusion.19 = f32[512,512]{1,0:T(8,128)S(1)} fusion(f32[512,512]{1,0:T(8,128)S(1)} %fusion.99, f32[512,512]{1,0:T(8,128)S(1)} %fusion.103, f32[512,512]{1,0:T(8,128)S(1)} %fusion.107, f32[512,512]{1,0:T(8,128)S(1)} %fusion.111, f32[512,512]{1,0:T(8,128)S(1)} %fusion.115, f32[512,512]{1,0:T(8,128)S(1)} %fusion.119, f32[512,512]{1,0:T(8,128)S(1)} %fusion.123, ...), kind=kOutput, calls=%fused_computation.66 | convolution fusion | flops 138936320 | bytes 20447232 | tf_op jit(solution)/shard_map/dot_general | solution.py:108
  42.4 1.3 %convolution_add_fusion.1 = f32[512,512]{1,0:T(8,128)} fusion(f32[512,512]{1,0:T(8,128)S(1)} %convolution_add_fusion.2, bf16[512,256]{1,0:T(8,128)(2,1)S(1)} %bitcast.365, bf16[3,3,3,512,256]{4,3,2,1,0:T(8,128)(2,1)S(1)} %bitcast.323), kind=kOutput, calls=%fused_computation.41 | convolution fusion | flops 134479872 | bytes 2621440 | tf_op jit(solution)/shard_map/dot_general | solution.py:108
  43.7 8.4 %all-to-all-done = bf16[8,1,1,6,18,512]{5,4,3,2,1,0:T(8,128)(2,1)} async-done(((bf16[8,1,1,6,18,512]{5,4,3,2,1,0:T(8,128)(2,1)}), bf16[8,1,1,6,18,512]{5,4,3,2,1,0:T(8,128)(2,1)}, u32[]{:S(2)}, u32[]{:S(2)}) %all-to-all-start) | async-done | bytes 884768 | tf_op jit(solution)/shard_map/all_to_all | solution.py:12
  52.1 1.6 %fusion = f32[8,6,18]{2,1,0:T(8,128)S(1)} fusion(bf16[8,1,1,6,18,512]{5,4,3,2,1,0:T(8,128)(2,1)} %all-to-all-done), kind=kLoop, calls=%fused_computation.36 | loop fusion | flops 1326240 | bytes 888192 | tf_op jit(solution)/shard_map/reduce_sum | solution.py:36
  53.7 2.0 %broadcast_multiply_fusion = (f32[8,6,18,512]{3,2,1,0:T(8,128)S(1)}, bf16[8,6,18,512]{3,2,1,0:T(8,128)(2,1)S(1)}, f32[8,6,18,512]{3,2,1,0:T(8,128)S(1)}) fusion(f32[512]{0:T(512)S(1)} %copy-done.3, f32[8,6,18]{2,1,0:T(8,128)S(1)} %get-tuple-element.69, bf16[8,1,1,6,18,512]{5,4,3,2,1,0:T(8,128)(2,1)} %all-to-all-done), kind=kLoop, calls=%fused_computation.98 | loop fusion | flops 3538944 | bytes 5313920 | tf_op jit(solution)/shard_map/mul | solution.py:39
  57.7 3.7 %collective-permute-start = (bf16[2,6,18,512]{3,2,1,0:T(8,128)(2,1)S(1)}, bf16[2,6,18,512]{3,2,1,0:T(8,128)(2,1)S(1)}, u32[]{:S(2)}, u32[]{:S(2)}) collective-permute-start(bf16[2,6,18,512]{3,2,1,0:T(8,128)(2,1)S(1)} %slice.398), channel_id=1, source_target_pairs={{0,8},{1,9},{2,10},{3,11},{4,12},{5,13},{6,14},{7,15},{16,24},{17,... | collective-permute-start | bytes 663560 | tf_op jit(solution)/shard_map/ppermute | solution.py:32
  61.5 1.3 %slice.397 = bf16[8,4,16,512]{3,2,1,0:T(8,128)(2,1)S(1)} slice(bf16[8,6,18,512]{3,2,1,0:T(8,128)(2,1)} %bitcast.12), slice={[0:8], [1:5], [1:17], [0:512]} | slice | bytes 1048576 | tf_op jit(solution)/shard_map/slice | solution.py:75
  63.1 1.6 %fusion.21 = bf16[8,1,4,16,512]{4,3,2,1,0:T(8,128)(2,1)} fusion(f32[8,6,18,512]{3,2,1,0:T(8,128)S(1)} %get-tuple-element.30, f32[8,4,16]{2,1,0:T(4,128)S(1)} %broadcast_multiply_fusion.1, f32[8,4,16]{2,1,0:T(4,128)S(1)} %slice_bitcast_fusion.8, bf16[512,256]{1,0:T(8,128)(2,1)S(1)} %copy-done, bf16[8,1,4,16,256]{4,3,2,1,0:T(8,128)(2,1)S(1)} %copy-done.2, ...), kind=kOutput, calls=%fused_computation.68 | convolution fusion | flops 137887744 | bytes 4200448 | tf_op jit(solution)/shard_map/dot_general | solution.py:96
  65.3 1.9 %collective-permute-done = bf16[2,6,18,512]{3,2,1,0:T(8,128)(2,1)S(1)} collective-permute-done((bf16[2,6,18,512]{3,2,1,0:T(8,128)(2,1)S(1)}, bf16[2,6,18,512]{3,2,1,0:T(8,128)(2,1)S(1)}, u32[]{:S(2)}, u32[]{:S(2)}) %collective-permute-start) | collective-permute-done | bytes 221216 | tf_op jit(solution)/shard_map/ppermute | solution.py:32
  67.2 1.1 %fusion.48 = (bf16[8,4,16,512]{3,2,1,0:T(8,128)(2,1)S(1)}, bf16[8,4,16,512]{3,2,1,0:T(8,128)(2,1)S(1)}, bf16[8,4,16,512]{3,2,1,0:T(8,128)(2,1)S(1)}, bf16[8,4,16...) fusion(bf16[8,6,18,512]{3,2,1,0:T(8,128)(2,1)S(1)} %get-tuple-e, ...), kind=kLoop, calls=%fused_computation.126 | loop fusion | flops 2359296 | bytes 7241728 | tf_op jit(solution)/shard_map/concatenate | solution.py:77
  70.5 1.3 %fusion.56 = (bf16[8,4,16,512]{3,2,1,0:T(8,128)(2,1)S(1)}, bf16[8,4,16,512]{3,2,1,0:T(8,128)(2,1)S(1)}, bf16[8,4,16,512]{3,2,1,0:T(8,128)(2,1)S(1)}, bf16[8,4,16...) fusion(bf16[8,6,18,512]{3,2,1,0:T(8,128)(2,1)S(1)} %get-tuple-e, ...), kind=kLoop, calls=%fused_computation.134 | loop fusion | flops 9437184 | bytes 7241728 | tf_op jit(solution)/shard_map/concatenate | solution.py:77
  74.7 0.8 fusion.38
  77.7 1.0 %fusion.39 = bf16[512,256]{1,0:T(8,128)(2,1)} fusion(f32[512,256]{1,0:T(8,128)S(1)} %convolution_add_fusion.9, bf16[512,512]{1,0:T(8,128)(2,1)S(1)} %bitcast.340, bf16[3,3,3,512,256]{4,3,2,1,0:T(8,128)(2,1)S(1)} %bitcast.325), kind=kOutput, calls=%fused_computation.96 | convolution fusion | flops 134479872 | bytes 1572864 | tf_op jit(solution)/shard_map/dot_general | solution.py:85
  (93 shorter events, 25.1 us)
Async XLA Ops:
  0.6 62.2 %copy-start = (bf16[512,256]{1,0:T(8,128)(2,1)S(1)}, bf16[512,256]{1,0:T(8,128)(2,1)}, u32[]{:S(2)}) copy-start(bf16[512,256]{1,0:T(8,128)(2,1)} %param.8) | copy-start | bytes 786436
  1.7 22.2 %collective-permute-start.1 = (bf16[8,4,1,256]{3,2,1,0:T(2,128)(2,1)S(1)}, bf16[8,4,1,256]{3,2,1,0:T(2,128)(2,1)S(1)}, u32[]{:S(2)}, u32[]{:S(2)}) collective-permute-start(bf16[8,4,1,256]{3,2,1,0:T(2,128)(2,1)S(1)} %get-tuple-element.66), channel_id=1, source_target_pairs={{0,1},{1,2},{2,3},{3,4},{4,5},{5,6},{6,7},{8,9},{9,10},{10,11},{11... | collective-permute-start | bytes 49160 | tf_op jit(solution)/shard_map/ppermute | solution.py:21
  4.1 19.8 %collective-permute-start.2 = (bf16[8,4,1,256]{3,2,1,0:T(2,128)(2,1)S(1)}, bf16[8,4,1,256]{3,2,1,0:T(2,128)(2,1)S(1)}, u32[]{:S(2)}, u32[]{:S(2)}) collective-permute-start(bf16[8,4,1,256]{3,2,1,0:T(2,128)(2,1)S(1)} %get-tuple-element.67), channel_id=1, source_target_pairs={{1,0},{2,1},{3,2},{4,3},{5,4},{6,5},{7,6},{9,8},{10,9},{11,10},{12... | collective-permute-start | bytes 49160 | tf_op jit(solution)/shard_map/ppermute | solution.py:24
  8.8 13.8 %copy-start.2 = (bf16[8,1,4,16,256]{4,3,2,1,0:T(8,128)(2,1)S(1)}, bf16[8,1,4,16,256]{4,3,2,1,0:T(8,128)(2,1)}, u32[]{:S(2)}) copy-start(bf16[8,1,4,16,256]{4,3,2,1,0:T(8,128)(2,1)} %param.9) | copy-start | bytes 786436
  14.1 18.9 %slice-start = ((s8[7077888]{0:T(1024)(128)(4,1)}), s8[2883584]{0:T(1024)(128)(4,1)S(1)}, s32[]{:S(2)}) async-start(s8[7077888]{0:T(1024)(128)(4,1)} %bitcast.322), calls=%async_computation.1 | async-start | bytes 5767168
  14.1 38.0 %all-to-all-start = ((bf16[8,1,1,6,18,512]{5,4,3,2,1,0:T(8,128)(2,1)}), bf16[8,1,1,6,18,512]{5,4,3,2,1,0:T(8,128)(2,1)}, u32[]{:S(2)}, u32[]{:S(2)}) async-start(bf16[8,1,1,6,18,512]{5,4,3,2,1,0:T(8,128)(2,1)} %fusion.226), calls=%async_computation | async-start | bytes 2359296 | tf_op jit(solution)/shard_map/all_to_all | solution.py:12
  24.4 8.2 %collective-permute-start.3 = (bf16[2,6,18,256]{3,2,1,0:T(8,128)(2,1)S(1)}, bf16[2,6,18,256]{3,2,1,0:T(8,128)(2,1)S(1)}, u32[]{:S(2)}, u32[]{:S(2)}) collective-permute-start(bf16[2,6,18,256]{3,2,1,0:T(8,128)(2,1)S(1)} %slice.445), channel_id=1, source_target_pairs={{8,0},{9,1},{10,2},{11,3},{12,4},{13,5},{14,6},{15,7},{24,16},{25,... | collective-permute-start | bytes 331784 | tf_op jit(solution)/shard_map/ppermute | solution.py:32
  25.7 7.4 %slice-start.1 = ((s8[7077888]{0:T(1024)(128)(4,1)}), s8[4194304]{0:T(1024)(128)(4,1)S(1)}, s32[]{:S(2)}) async-start(s8[7077888]{0:T(1024)(128)(4,1)} %bitcast.322), calls=%async_computation.2 | async-start | bytes 8388608
  42.4 11.3 %copy-start.3 = (f32[512]{0:T(512)S(1)}, f32[512]{0:T(512)}, u32[]{:S(2)}) copy-start(f32[512]{0:T(512)} %param.6) | copy-start | bytes 6148
  55.8 1.2 %copy-start.1 = (f32[512,512]{1,0:T(8,128)S(1)}, f32[512,512]{1,0:T(8,128)}, u32[]{:S(2)}) copy-start(f32[512,512]{1,0:T(8,128)} %convolution_add_fusion.1) | copy-start | bytes 3145732
  57.0 7.7 %slice-start.2 = ((s8[7077888]{0:T(1024)(128)(4,1)}), s8[4194304]{0:T(1024)(128)(4,1)S(1)}, s32[]{:S(2)}) async-start(s8[7077888]{0:T(1024)(128)(4,1)} %bitcast.324), calls=%async_computation.3 | async-start | bytes 8388608
  57.7 9.5 %collective-permute-start = (bf16[2,6,18,512]{3,2,1,0:T(8,128)(2,1)S(1)}, bf16[2,6,18,512]{3,2,1,0:T(8,128)(2,1)S(1)}, u32[]{:S(2)}, u32[]{:S(2)}) collective-permute-start(bf16[2,6,18,512]{3,2,1,0:T(8,128)(2,1)S(1)} %slice.398), channel_id=1, source_target_pairs={{0,8},{1,9},{2,10},{3,11},{4,12},{5,13},{6,14},{7,15},{16,24},{17,... | collective-permute-start | bytes 663560 | tf_op jit(solution)/shard_map/ppermute | solution.py:32
  63.1 1.9 %slice-start.3 = ((s8[7077888]{0:T(1024)(128)(4,1)}), s8[2883584]{0:T(1024)(128)(4,1)S(1)}, s32[]{:S(2)}) async-start(s8[7077888]{0:T(1024)(128)(4,1)} %bitcast.324), calls=%async_computation.4 | async-start | bytes 5767168
